TPU v7x, 32 devices: a whole 2x2x4 slice. The times are simulated.
32 devices in a mesh: img: 8 (over z, y), txt: 4 (over x, core).
Axes of the slice: x: 2, y: 2, z: 4, core: 2. Of those that a mesh axis runs over, the one named last changes fastest.
Arguments:
- images: float32 [1024, 1024], P(('img', 'txt')), may hold values from -1 to 1
- texts: float32 [1024, 1024], P(('txt', 'img')), may hold values from -1 to 1
- labels: int32 [1024], P('img'), may hold values from 0 to 1023, each once
Outputs:
- row_loss: float32 [1024], P('img')
- image_grad: float32 [1024, 1024], P(('img', 'txt'))
- text_grad: float32 [1024, 1024], P(('txt', 'img'))
Inputs may be any that keep to these rules, and one draw needn't show every extreme that they name: `labels`: each text index appears exactly once.
All inputs are finite; a program needn't handle non-finite values.
Results may differ from a plain program's by a relative error of at most 0.017.
Values may be sent and summed in bfloat16 or wider, within the bound.
A program may use at most 64 MiB of HBM per device.

v0:
```python
import jax
import jax.numpy as jnp
from jax import lax
from jax.sharding import PartitionSpec as P

logit_scale = 100.0


def merged(part, axis, combine):
    gathered = jax.tree.map(lambda a: lax.all_gather(a, axis), part)

    def take(source):
        return jax.tree.map(lambda a: lax.dynamic_index_in_dim(a, source, 0, False), gathered)

    return lax.fori_loop(
        1, lax.axis_size(axis), lambda source, state: combine(state, take(source)), take(0)
    )


def combine(earlier, later):
    highest = jnp.maximum(earlier[0], later[0])
    total = earlier[1] * jnp.exp(earlier[0] - highest) + later[1] * jnp.exp(later[0] - highest)
    return (highest, total, earlier[2] + later[2])


def local(images, texts, labels):
    img_panel = lax.all_gather(images.astype(jnp.bfloat16), "txt", axis=0, tiled=True)
    txt_panel = lax.all_gather(texts.astype(jnp.bfloat16), "img", axis=0, tiled=True)
    text_rows = txt_panel.shape[0]
    logits = logit_scale * lax.dot_general(
        img_panel, txt_panel, (((1,), (1,)), ((), ())), preferred_element_type=jnp.float32
    )
    columns = lax.axis_index("txt") * text_rows + lax.broadcasted_iota(jnp.int32, (1, text_rows), 1)
    hits = columns == labels[:, None]
    highest = jnp.max(logits, axis=1)
    exp_total = jnp.sum(jnp.exp(logits - highest[:, None]), axis=1)
    positive = jnp.sum(jnp.where(hits, logits, 0.0), axis=1)
    highest, exp_total, positive = merged((highest, exp_total, positive), "txt", combine)
    log_total = highest + jnp.log(exp_total)
    row_loss = log_total - positive
    grad_tile = (
        logit_scale * (jnp.exp(logits - log_total[:, None]) - hits.astype(jnp.float32))
    ).astype(jnp.bfloat16)
    terms = jnp.dot(grad_tile, txt_panel, preferred_element_type=jnp.float32)
    image_grad = lax.psum_scatter(
        terms.astype(jnp.bfloat16), "txt", scatter_dimension=0, tiled=True
    ).astype(jnp.float32)
    terms = lax.dot_general(
        grad_tile, img_panel, (((0,), (0,)), ((), ())), preferred_element_type=jnp.float32
    )
    text_grad = lax.psum_scatter(
        terms.astype(jnp.bfloat16), "img", scatter_dimension=0, tiled=True
    ).astype(jnp.float32)
    return (row_loss, image_grad, text_grad)


def solution(mesh):
    in_specs = (P(("img", "txt"), None), P(("txt", "img"), None), P("img"))
    out_specs = (P("img"), P(("img", "txt"), None), P(("txt", "img"), None))
    return jax.shard_map(local, mesh=mesh, in_specs=in_specs, out_specs=out_specs, check_vma=False)
```

profile of v0, /device:TPU:0, one launch (start us, length us, event | category | flops | bytes accessed | tf_op | source)
XLA Modules:
  0.0 161.3 jit_solution(13547509192258138272)
XLA Ops:
  7.2 0.0 reduce-scatter.3.cloned.1.call-start
  7.2 0.9 convert_element_type.24
  8.1 0.0 copy-start
  8.1 7.4 %all_gather.24 = bf16[128,1024]{1,0:T(8,128)(2,1)S(1)} all-gather(bf16[32,1024]{1,0:T(8,128)(2,1)S(1)} %convert_element_type.24), channel_id=1, replica_groups=mesh['img'=8,'txt'=4] {'txt'}, dimensions={0}, use_global_device_ids=true | all-gather | bytes 327680 | tf_op jit(solution)/shard_map/all_gather | solution.py:27
  15.5 0.0 copy-done
  15.5 31.9 %all_gather.25 = bf16[256,1024]{1,0:T(8,128)(2,1)S(1)} all-gather(bf16[32,1024]{1,0:T(8,128)(2,1)S(1)} %convert_element_type.25), channel_id=1, replica_groups=mesh['img'=8,'txt'=4] {'img'}, dimensions={0}, use_global_device_ids=true | all-gather | bytes 589824 | tf_op jit(solution)/shard_map/all_gather | solution.py:28
  47.4 0.4 fusion.15
  47.8 5.1 %all-gather.3 = f32[4,1,128]{2,1,0:T(1,128)S(1)} all-gather(f32[1,1,128]{2,1,0:T(1,128)S(1)} %bitcast.38), channel_id=2, replica_groups=mesh['img'=8,'txt'=4] {'txt'}, dimensions={0}, use_global_device_ids=true | all-gather | bytes 2560 | tf_op jit(solution)/shard_map/all_gather | solution.py:10
  52.9 0.0 copy-start.1
  52.9 0.7 copy-done.1
  53.6 0.2 fusion.7
  53.7 5.1 %all-gather.4 = f32[4,1,128]{2,1,0:T(1,128)S(1)} all-gather(f32[1,1,128]{2,1,0:T(1,128)S(1)} %bitcast.40), channel_id=3, replica_groups=mesh['img'=8,'txt'=4] {'txt'}, dimensions={0}, use_global_device_ids=true | all-gather | bytes 2560 | tf_op jit(solution)/shard_map/all_gather | solution.py:10
  58.8 5.0 %all-gather.5 = f32[4,1,128]{2,1,0:T(1,128)S(1)} all-gather(f32[1,1,128]{2,1,0:T(1,128)S(1)} %bitcast.39), channel_id=4, replica_groups=mesh['img'=8,'txt'=4] {'txt'}, dimensions={0}, use_global_device_ids=true | all-gather | bytes 2560 | tf_op jit(solution)/shard_map/all_gather | solution.py:10
  63.9 0.1 while.19
  64.0 0.5 fusion.14
  64.5 1.0 convolution_convert_fusion.1
  65.5 0.0 reduce-scatter.3.cloned.1.call-update
  65.5 0.0 reduce-scatter.5.cloned.1.call-start
  65.6 1.2 convolution_convert_fusion
  66.8 0.0 reduce-scatter.5.cloned.1.call-update
  66.8 19.7 %reduce-scatter.3.cloned.1.call-done = bf16[32,1024]{1,0:T(8,128)(2,1)} async-done(((bf16[128,1024]{1,0:T(8,128)(2,1)}), bf16[32,1024]{1,0:T(8,128)(2,1)}) %reduce-scatter.3.cloned.1.call-update) | async-done | bytes 65552 | tf_op jit(solution)/shard_map/reduce_scatter | solution.py:45
  86.5 1.5 convert_element_type.29
  88.0 65.0 %reduce-scatter.5.cloned.1.call-done = bf16[32,1024]{1,0:T(8,128)(2,1)} async-done(((bf16[256,1024]{1,0:T(8,128)(2,1)}), bf16[32,1024]{1,0:T(8,128)(2,1)}) %reduce-scatter.5.cloned.1.call-update) | async-done | bytes 65552 | tf_op jit(solution)/shard_map/reduce_scatter | solution.py:51
  152.9 1.5 convert_element_type.31
  (8 shorter events, 0.1 us)
Async XLA Ops:
  7.2 79.3 %reduce-scatter.3.cloned.1.call-start = ((), (), s32[]{:S(2)}) async-start(), calls=%async_computation.2 | async-start | bytes 327680 | tf_op jit(solution)/shard_map/reduce_scatter | solution.py:45
  8.1 7.4 %copy-start = (f32[32,1024]{1,0:T(8,128)S(1)}, f32[32,1024]{1,0:T(8,128)}, u32[]{:S(2)}) copy-start(f32[32,1024]{1,0:T(8,128)} %param.6) | copy-start | bytes 393220
  52.9 0.7 copy-start.1
  65.5 87.4 %reduce-scatter.5.cloned.1.call-start = ((), (), s32[]{:S(2)}) async-start(), calls=%async_computation.3 | async-start | bytes 589824 | tf_op jit(solution)/shard_map/reduce_scatter | solution.py:51
Sparse Core Ops, SparseCore 0:
  65.6 20.7 reduce-scatter.2
  89.8 63.0 reduce-scatter.4
where the time goes:
time: 162 us; the launch traced here: 161 us
  waiting for transfers between devices  84.7 us (52%)
  blocking collectives  54.5 us (34%)
  between operations  14.1 us (9%)
  other arithmetic  4.71 us (3%)
  matrix products  2.58 us (2%)
    reduce_scatter x1, waiting for transfers between devices, local(): lax.psum_scatter(terms.astype(jnp.bfloat16), 'img', scatter_dimension=0,...  65 us
    all_gather x1, blocking collectives, local(): lax.all_gather(texts.astype(jnp.bfloat16), 'img', axis=0, tiled=True)  31.9 us
    reduce_scatter x1, waiting for transfers between devices, local(): lax.psum_scatter(terms.astype(jnp.bfloat16), 'txt', scatter_dimension=0,...  19.7 us
    all_gather x3, blocking collectives, merged(): gathered = jax.tree.map(lambda a: lax.all_gather(a, axis), part)  15.2 us
    all_gather x1, blocking collectives, local(): lax.all_gather(images.astype(jnp.bfloat16), 'txt', axis=0, tiled=True)  7.35 us
  transfers between devices with their start and end apart: 2, of which 2 were waited for; matrix products, arithmetic and copies ran while one was open for 2% of the time, Pallas kernels for 0%

commit v1 on v0

v1 whole, which is shorter than its diff:
```python
import functools

import jax
import jax.numpy as jnp
from jax import lax
from jax.experimental import pallas as pl
from jax.experimental.pallas import tpu as pltpu
from jax.sharding import PartitionSpec as P

logit_scale = 100.0
MESH = pl.DeviceIdType.MESH


def kernel(
    n_img, n_txt,
    labels_ref, images_hbm, texts_hbm,
    loss_ref, image_grad_ref, text_grad_ref,
    images_in, texts_in, img_panel, txt_panel, stats, text_terms, from_pair, paired,
    from_line, image_terms, from_txt,
    load_sems, send_sems, txt_sems, img_sems, stat_sems, pair_sems, line_sems, term_sems,
):
    length = n_img // 2
    rows, width = images_in.shape
    img, txt = lax.axis_index("img"), lax.axis_index("txt")
    z, y = img // 2, img % 2
    c = txt % 2
    across = (z * 2 + (1 - y), txt)
    partner = (img, txt - c + (1 - c))
    up, down = ((z + 1) * 2 + y, txt), ((z - 1) * 2 + y, txt)
    has_up, has_down = z < length - 1, z > 0

    loads = [
        pltpu.make_async_copy(images_hbm, images_in, load_sems.at[0]),
        pltpu.make_async_copy(texts_hbm, texts_in, load_sems.at[1]),
    ]
    for load in loads:
        load.start()

    barrier = pltpu.get_barrier_semaphore()
    others = [(img, lax.rem(txt + k, n_txt)) for k in range(1, n_txt)]
    for device in [across] + others:
        pl.semaphore_signal(barrier, inc=1, device_id=device, device_id_type=MESH)

    @pl.when(has_up)
    def _():
        pl.semaphore_signal(barrier, inc=1, device_id=up, device_id_type=MESH)

    @pl.when(has_down)
    def _():
        pl.semaphore_signal(barrier, inc=1, device_id=down, device_id_type=MESH)

    loads[1].wait()
    txt_panel[0, z] = texts_in[...].astype(jnp.bfloat16)
    loads[0].wait()
    img_panel[txt] = images_in[...].astype(jnp.bfloat16)
    pl.semaphore_wait(barrier, n_txt + jnp.where(has_up, 1, 0) + jnp.where(has_down, 1, 0))

    sent = []

    def guarded(condition, act):
        if condition is None:
            act()
        else:
            pl.when(condition)(act)

    def push(src, dst, arrival, device, condition=None):
        number = len(sent)

        def copy():
            return pltpu.make_async_remote_copy(
                src_ref=src(), dst_ref=dst(), send_sem=send_sems.at[number], recv_sem=arrival(),
                device_id=device, device_id_type=MESH,
            )

        sent.append((condition, copy))
        guarded(condition, lambda: copy().start())

    def arrived(ref, arrival, condition=None):
        def act():
            pltpu.make_async_remote_copy(
                src_ref=ref(), dst_ref=ref(), send_sem=send_sems.at[0], recv_sem=arrival(),
                device_id=across, device_id_type=MESH,
            ).wait_recv()

        guarded(condition, act)

    def push_text(source, side, device, condition=None):
        push(
            lambda: txt_panel.at[0, source], lambda: txt_panel.at[side, source],
            lambda: txt_sems.at[side, source], device, condition,
        )

    def push_image(source, device):
        push(
            lambda: img_panel.at[source], lambda: img_panel.at[source],
            lambda: img_sems.at[source], device,
        )

    def image_arrived(source):
        arrived(lambda: img_panel.at[source], lambda: img_sems.at[source])

    push_text(z, 0, up, has_up)
    push_text(z, 0, down, has_down)
    push_text(z, 1, across)
    same_side = [lax.rem(txt + 2 * k, n_txt) for k in range(1, n_txt // 2)]
    for other in same_side:
        push_image(txt, (img, other))
    push_image(txt, partner)

    for step in range(1, length):
        for source, onward, more in ((z - step, up, has_up), (z + step, down, has_down)):
            there = jnp.logical_and(source >= 0, source < length)
            arrived(
                lambda source=source: txt_panel.at[0, source],
                lambda source=source: txt_sems.at[0, source], there,
            )
            push_text(source, 0, onward, jnp.logical_and(there, more))
            push_text(source, 1, across, there)
        if step == 1:
            for other in same_side:
                image_arrived(other)
                push_image(other, partner)
    image_arrived(partner[1])
    for other in same_side:
        image_arrived(other - c + (1 - c))
    for source in range(length):
        arrived(lambda: txt_panel.at[1, source], lambda: txt_sems.at[1, source])

    text_rows, image_rows = n_img * rows, n_txt * rows
    image_low = img_panel[...].reshape(image_rows, width)
    text_low = txt_panel[...].reshape(text_rows, width)
    logits = logit_scale * lax.dot_general(
        text_low, image_low, (((1,), (1,)), ((), ())), preferred_element_type=jnp.float32
    )
    place = lax.broadcasted_iota(jnp.int32, (text_rows, 1), 0)
    side = place // (length * rows)
    block = (place // rows) % length
    column = txt * text_rows + (block * 2 + jnp.where(side == 0, y, 1 - y)) * rows + place % rows
    hits = column == labels_ref[...]
    highest = jnp.max(logits, axis=0, keepdims=True)
    exp_total = jnp.sum(jnp.exp(logits - highest), axis=0, keepdims=True)
    positive = jnp.sum(jnp.where(hits, logits, 0.0), axis=0, keepdims=True)
    line = lax.broadcasted_iota(jnp.int32, stats.shape[1:], 0)
    stats[txt] = jnp.where(
        line == 0, highest, jnp.where(line == 1, exp_total, jnp.where(line == 2, positive, 0.0))
    )
    for device in others:
        push(
            lambda: stats.at[txt], lambda: stats.at[txt], lambda: stat_sems.at[txt], device
        )
    for device in others:
        arrived(lambda: stats.at[device[1]], lambda: stat_sems.at[device[1]])
    every = stats[...]
    tops = every[:, 0:1, :]
    top = jnp.max(tops, axis=0)
    total = jnp.sum(every[:, 1:2, :] * jnp.exp(tops - top[None]), axis=0)
    log_total = top + jnp.log(total)
    loss_ref[...] = log_total - jnp.sum(every[:, 2:3, :], axis=0)
    grad_tile = (
        logit_scale * (jnp.exp(logits - log_total) - hits.astype(jnp.float32))
    ).astype(jnp.bfloat16)

    half = length * rows

    def side_terms(side):
        text_terms[side] = (
            jnp.dot(
                grad_tile[side * half : (side + 1) * half], image_low,
                preferred_element_type=jnp.float32,
            )
            .astype(jnp.bfloat16)
            .reshape(length, rows, width)
        )

    far_first = []
    for step in range(length - 1, 0, -1):
        for target in (z + step, z - step):
            far_first.append((target, jnp.logical_and(target >= 0, target < length)))
    side_terms(1)
    for target, there in far_first + [(z, None)]:
        push(
            lambda target=target: text_terms.at[1, target],
            lambda target=target: from_pair.at[target],
            lambda target=target: pair_sems.at[target], across, there,
        )
    image_terms[...] = (
        lax.dot_general(
            grad_tile, text_low, (((0,), (0,)), ((), ())), preferred_element_type=jnp.float32
        )
        .astype(jnp.bfloat16)
        .reshape(n_txt, rows, width)
    )
    for device in others:
        push(
            lambda device=device: image_terms.at[device[1]], lambda: from_txt.at[txt],
            lambda: term_sems.at[txt], device,
        )
    side_terms(0)

    def pair_sum(target):
        return text_terms[0, target].astype(jnp.float32) + from_pair[target].astype(jnp.float32)

    for target, there in far_first:
        arrived(
            lambda target=target: from_pair.at[target],
            lambda target=target: pair_sems.at[target], there,
        )

        def add(target=target):
            paired[target] = pair_sum(target).astype(jnp.bfloat16)

        guarded(there, add)
        push(
            lambda target=target: paired.at[target], lambda: from_line.at[z],
            lambda: line_sems.at[z], (target * 2 + y, txt), there,
        )

    for device in others:
        arrived(lambda: from_txt.at[device[1]], lambda: term_sems.at[device[1]])
    image_sum = image_terms[txt].astype(jnp.float32)
    for device in others:
        image_sum += from_txt[device[1]].astype(jnp.float32)
    image_grad_ref[...] = image_sum

    arrived(lambda: from_pair.at[z], lambda: pair_sems.at[z])
    text_grad_ref[...] = pair_sum(z)
    for source, there in far_first[::-1]:
        def add(source=source):
            arrived(lambda: from_line.at[source], lambda: line_sems.at[source])
            text_grad_ref[...] += from_line[source].astype(jnp.float32)

        guarded(there, add)

    for condition, copy in sent:
        guarded(condition, lambda: copy().wait_send())


def local(n_img, n_txt, images, texts, labels):
    rows, width = images.shape
    length = n_img // 2
    image_rows = labels.shape[0]
    vmem = pl.BlockSpec(memory_space=pltpu.VMEM)
    hbm = pl.BlockSpec(memory_space=pl.ANY)
    low = jnp.bfloat16
    dma = pltpu.SemaphoreType.DMA
    sends = 3 + n_txt + 4 * length + 2 * (n_txt - 1) + 4 * length + n_txt
    loss, image_grad, text_grad = pl.pallas_call(
        functools.partial(kernel, n_img, n_txt),
        out_shape=(
            jax.ShapeDtypeStruct((1, image_rows), jnp.float32),
            jax.ShapeDtypeStruct((rows, width), jnp.float32),
            jax.ShapeDtypeStruct((rows, width), jnp.float32),
        ),
        in_specs=[vmem, hbm, hbm],
        out_specs=(vmem, vmem, vmem),
        scratch_shapes=[
            pltpu.VMEM((rows, width), jnp.float32),
            pltpu.VMEM((rows, width), jnp.float32),
            pltpu.VMEM((n_txt, rows, width), low),
            pltpu.VMEM((2, length, rows, width), low),
            pltpu.VMEM((n_txt, 8, image_rows), jnp.float32),
            pltpu.VMEM((2, length, rows, width), low),
            pltpu.VMEM((length, rows, width), low),
            pltpu.VMEM((length, rows, width), low),
            pltpu.VMEM((length, rows, width), low),
            pltpu.VMEM((n_txt, rows, width), low),
            pltpu.VMEM((n_txt, rows, width), low),
            dma((2,)),
            dma((sends,)),
            dma((2, length)),
            dma((n_txt,)),
            dma((n_txt,)),
            dma((length,)),
            dma((length,)),
            dma((n_txt,)),
        ],
        compiler_params=pltpu.CompilerParams(
            collective_id=0, has_side_effects=True, vmem_limit_bytes=48 * 1024 * 1024
        ),
    )(labels.reshape(1, image_rows), images, texts)
    return loss.reshape(image_rows), image_grad, text_grad


def solution(mesh):
    in_specs = (P(("img", "txt"), None), P(("txt", "img"), None), P("img"))
    out_specs = (P("img"), P(("img", "txt"), None), P(("txt", "img"), None))
    body = functools.partial(local, mesh.shape["img"], mesh.shape["txt"])
    return jax.shard_map(body, mesh=mesh, in_specs=in_specs, out_specs=out_specs, check_vma=False)
```

time: 162 us -> 36.3 us (0.22)
  waiting for transfers between devices: 84.7 us -> 0 us
  blocking collectives: 54.5 us -> 0 us
  Pallas kernels: 0 us -> 31.2 us
  between operations: 14.1 us -> 0.65 us
  other arithmetic: 4.71 us -> 0 us
  local copies, waits for them, and re-layouts: 0.66 us -> 4.28 us
  matrix products: 2.58 us -> 0 us
    reduce_scatter x2 -> x0, waiting for transfers between devices: 84.6 us -> none  [the longest x1 65 us: local(): lax.psum_scatter(terms.astype(jnp.bfloat16), 'img', scatter_dimension=0,...]
    all_gather x5 -> x0, blocking collectives: 54.5 us -> none  [the longest x1 31.9 us: local(): lax.all_gather(texts.astype(jnp.bfloat16), 'img', axis=0, tiled=True)]
    pallas_call x0 -> x1, Pallas kernels: none -> 31.2 us  [local(): pl.pallas_call(functools.partial(kernel, n_img, n_txt), out_shape=(jax.Sh...]
    convert_element_type x4 -> x0, other arithmetic: 3.93 us -> none  [the longest x1 1.5 us: local(): image_grad = lax.psum_scatter(terms.astype(jnp.bfloat16), 'txt', scatter_...]
    unnamed x4 -> x9, local copies, waits for them, and re-layouts: 0.66 us -> 4.28 us
    dot_general x3 -> x0, matrix products: 2.58 us -> none  [the longest x1 1.2 us: local(): lax.dot_general(grad_tile, img_panel, (((0,), (0,)), ((), ())), preferred...]
  transfers between devices with their start and end apart: 2 -> 0, of which waited for: 2 -> 0; matrix products, arithmetic and copies ran while one was open for 2% -> 0% of each run, Pallas kernels for 0% -> 0%
where the time goes in v1:
time: 36.3 us; the launch traced here: 36.2 us
  Pallas kernels  31.2 us (86%)
  local copies, waits for them, and re-layouts  4.28 us (12%)
  between operations  0.65 us (2%)
    pallas_call x1, Pallas kernels, local(): pl.pallas_call(functools.partial(kernel, n_img, n_txt), out_shape=(jax.Sh...  31.2 us
    unnamed x9, local copies, waits for them, and re-layouts  4.28 us

profile of v1, /device:TPU:0, one launch (start us, length us, event | category | flops | bytes accessed | tf_op | source)
XLA Modules:
  0.0 36.2 jit_solution(15301728587486851156)
XLA Ops:
  0.6 0.0 copy-start.2
  0.6 0.6 %copy-done.2 = s32[128]{0:T(128)S(1)} copy-done((s32[128]{0:T(128)S(1)}, s32[128]{0:T(128)}, u32[]{:S(2)}) %copy-start.2) | copy-done | bytes 536
  1.3 0.0 copy-start
  1.3 0.9 %copy-done = f32[32,1024]{1,0:T(8,128)S(1)} copy-done((f32[32,1024]{1,0:T(8,128)S(1)}, f32[32,1024]{1,0:T(8,128)}, u32[]{:S(2)}) %copy-start) | copy-done | bytes 131096
  2.2 0.0 copy-start.1
  2.2 0.9 %copy-done.1 = f32[32,1024]{1,0:T(8,128)S(1)} copy-done((f32[32,1024]{1,0:T(8,128)S(1)}, f32[32,1024]{1,0:T(8,128)}, u32[]{:S(2)}) %copy-start.1) | copy-done | bytes 131096
  3.1 31.2 %shard_map.58 = (f32[1,128]{1,0:T(1,128)S(1)}, f32[32,1024]{1,0:T(8,128)S(1)}, f32[32,1024]{1,0:T(8,128)S(1)}) custom-call(s32[1,128]{1,0:T(1,128)S(1)} %bitcast.2, f32[32,1024]{1,0:T(8,128)S(1)} %copy-done, f32[32,1024]{1,0:T(8,128)S(1)} %copy-done.1), custom_call_target="tpu_custom_call" | custom-call | tf_op jit(solution)/shard_map/pallas_call | solution.py:247
  34.3 0.5 %copy.9 = f32[128]{0:T(128)} copy(f32[128]{0:T(128)S(1)} %bitcast.3) | data formatting | bytes 1024
  34.9 0.7 %copy.10 = f32[32,1024]{1,0:T(8,128)} copy(f32[32,1024]{1,0:T(8,128)S(1)} %get-tuple-element.13) | data formatting | bytes 262144
  35.5 0.7 %copy.11 = f32[32,1024]{1,0:T(8,128)} copy(f32[32,1024]{1,0:T(8,128)S(1)} %get-tuple-element.14) | data formatting | bytes 262144
Async XLA Ops:
  0.6 0.7 %copy-start.2 = (s32[128]{0:T(128)S(1)}, s32[128]{0:T(128)}, u32[]{:S(2)}) copy-start(s32[128]{0:T(128)} %param.5) | copy-start | bytes 1540
  1.3 0.9 %copy-start = (f32[32,1024]{1,0:T(8,128)S(1)}, f32[32,1024]{1,0:T(8,128)}, u32[]{:S(2)}) copy-start(f32[32,1024]{1,0:T(8,128)} %images_hbm.1) | copy-start | bytes 393220
  2.2 0.9 %copy-start.1 = (f32[32,1024]{1,0:T(8,128)S(1)}, f32[32,1024]{1,0:T(8,128)}, u32[]{:S(2)}) copy-start(f32[32,1024]{1,0:T(8,128)} %texts_hbm.1) | copy-start | bytes 393220

commit v2 on v1

--- a/solution.py
+++ b/solution.py
@@ -9,13 +9,14 @@
 
 logit_scale = 100.0
 MESH = pl.DeviceIdType.MESH
+parts = 2
 
 
 def kernel(
     n_img, n_txt,
-    labels_ref, images_hbm, texts_hbm,
+    labels_hbm, images_hbm, texts_hbm,
     loss_ref, image_grad_ref, text_grad_ref,
-    images_in, texts_in, img_panel, txt_panel, stats, text_terms, from_pair, paired,
+    labels_ref, images_in, texts_in, img_panel, txt_panel, stats, text_terms, from_pair, paired,
     from_line, image_terms, from_txt,
     load_sems, send_sems, txt_sems, img_sems, stat_sems, pair_sems, line_sems, term_sems,
 ):
@@ -26,12 +27,13 @@
     c = txt % 2
     across = (z * 2 + (1 - y), txt)
     partner = (img, txt - c + (1 - c))
-    up, down = ((z + 1) * 2 + y, txt), ((z - 1) * 2 + y, txt)
-    has_up, has_down = z < length - 1, z > 0
+    piece = rows // parts
+    pieces = [pl.ds(part * piece, piece) for part in range(parts)]
 
     loads = [
         pltpu.make_async_copy(images_hbm, images_in, load_sems.at[0]),
         pltpu.make_async_copy(texts_hbm, texts_in, load_sems.at[1]),
+        pltpu.make_async_copy(labels_hbm, labels_ref, load_sems.at[2]),
     ]
     for load in loads:
         load.start()
@@ -41,19 +43,23 @@
     for device in [across] + others:
         pl.semaphore_signal(barrier, inc=1, device_id=device, device_id_type=MESH)
 
-    @pl.when(has_up)
-    def _():
-        pl.semaphore_signal(barrier, inc=1, device_id=up, device_id_type=MESH)
-
-    @pl.when(has_down)
-    def _():
-        pl.semaphore_signal(barrier, inc=1, device_id=down, device_id_type=MESH)
+    greeted = n_txt
+    for place in (z + 1, z - 1, z + 2, z - 2):
+        inside = jnp.logical_and(place >= 0, place < length)
+        greeted += jnp.where(inside, 1, 0)
+
+        @pl.when(inside)
+        def _():
+            pl.semaphore_signal(
+                barrier, inc=1, device_id=(place * 2 + y, txt), device_id_type=MESH
+            )
 
     loads[1].wait()
     txt_panel[0, z] = texts_in[...].astype(jnp.bfloat16)
     loads[0].wait()
     img_panel[txt] = images_in[...].astype(jnp.bfloat16)
-    pl.semaphore_wait(barrier, n_txt + jnp.where(has_up, 1, 0) + jnp.where(has_down, 1, 0))
+    loads[2].wait()
+    pl.semaphore_wait(barrier, greeted)
 
     sent = []
 
@@ -84,11 +90,26 @@
 
         guarded(condition, act)
 
-    def push_text(source, side, device, condition=None):
-        push(
-            lambda: txt_panel.at[0, source], lambda: txt_panel.at[side, source],
-            lambda: txt_sems.at[side, source], device, condition,
-        )
+    def push_text(source, part, side, device, condition=None):
+        push(
+            lambda: txt_panel.at[0, source, pieces[part]],
+            lambda: txt_panel.at[side, source, pieces[part]],
+            lambda: txt_sems.at[side, source, part], device, condition,
+        )
+
+    def text_arrived(source, part, side, condition=None):
+        arrived(
+            lambda: txt_panel.at[side, source, pieces[part]],
+            lambda: txt_sems.at[side, source, part], condition,
+        )
+
+    def pass_on(source, part, way, there=None):
+        for reach in (1, 2):
+            target = z + way * reach
+            inside = jnp.logical_and(target >= 0, target < length)
+            if there is not None:
+                inside = jnp.logical_and(inside, there)
+            push_text(source, part, 0, (target * 2 + y, txt), inside)
 
     def push_image(source, device):
         push(
@@ -99,23 +120,24 @@
     def image_arrived(source):
         arrived(lambda: img_panel.at[source], lambda: img_sems.at[source])
 
-    push_text(z, 0, up, has_up)
-    push_text(z, 0, down, has_down)
-    push_text(z, 1, across)
+    for part in range(parts):
+        push_text(z, part, 1, across)
+        for way in (1, -1):
+            pass_on(z, part, way)
     same_side = [lax.rem(txt + 2 * k, n_txt) for k in range(1, n_txt // 2)]
     for other in same_side:
         push_image(txt, (img, other))
     push_image(txt, partner)
 
     for step in range(1, length):
-        for source, onward, more in ((z - step, up, has_up), (z + step, down, has_down)):
-            there = jnp.logical_and(source >= 0, source < length)
-            arrived(
-                lambda source=source: txt_panel.at[0, source],
-                lambda source=source: txt_sems.at[0, source], there,
-            )
-            push_text(source, 0, onward, jnp.logical_and(there, more))
-            push_text(source, 1, across, there)
+        for part in range(parts):
+            for way in (1, -1):
+                source = z - way * step
+                there = jnp.logical_and(source >= 0, source < length)
+                text_arrived(source, part, 0, there)
+                if step % 2 == 0:
+                    pass_on(source, part, way, there)
+                push_text(source, part, 1, across, there)
         if step == 1:
             for other in same_side:
                 image_arrived(other)
@@ -124,7 +146,8 @@
     for other in same_side:
         image_arrived(other - c + (1 - c))
     for source in range(length):
-        arrived(lambda: txt_panel.at[1, source], lambda: txt_sems.at[1, source])
+        for part in range(parts):
+            text_arrived(source, part, 1)
 
     text_rows, image_rows = n_img * rows, n_txt * rows
     image_low = img_panel[...].reshape(image_rows, width)
@@ -177,12 +200,16 @@
         for target in (z + step, z - step):
             far_first.append((target, jnp.logical_and(target >= 0, target < length)))
     side_terms(1)
+    def push_pair(target, part, there):
+        push(
+            lambda: text_terms.at[1, target, pieces[part]],
+            lambda: from_pair.at[target, pieces[part]],
+            lambda: pair_sems.at[target, part], across, there,
+        )
+
     for target, there in far_first + [(z, None)]:
-        push(
-            lambda target=target: text_terms.at[1, target],
-            lambda target=target: from_pair.at[target],
-            lambda target=target: pair_sems.at[target], across, there,
-        )
+        for part in range(parts):
+            push_pair(target, part, there)
     image_terms[...] = (
         lax.dot_general(
             grad_tile, text_low, (((0,), (0,)), ((), ())), preferred_element_type=jnp.float32
@@ -197,23 +224,31 @@
         )
     side_terms(0)
 
-    def pair_sum(target):
-        return text_terms[0, target].astype(jnp.float32) + from_pair[target].astype(jnp.float32)
+    def pair_sum(target, part):
+        return text_terms[0, target, pieces[part]].astype(jnp.float32) + from_pair[
+            target, pieces[part]
+        ].astype(jnp.float32)
+
+    def pair_arrived(target, part, there=None):
+        arrived(
+            lambda: from_pair.at[target, pieces[part]],
+            lambda: pair_sems.at[target, part], there,
+        )
+
+    def push_line(target, part, there):
+        def add():
+            paired[target, pieces[part]] = pair_sum(target, part).astype(jnp.bfloat16)
+
+        pair_arrived(target, part, there)
+        guarded(there, add)
+        push(
+            lambda: paired.at[target, pieces[part]], lambda: from_line.at[z, pieces[part]],
+            lambda: line_sems.at[z, part], (target * 2 + y, txt), there,
+        )
 
     for target, there in far_first:
-        arrived(
-            lambda target=target: from_pair.at[target],
-            lambda target=target: pair_sems.at[target], there,
-        )
-
-        def add(target=target):
-            paired[target] = pair_sum(target).astype(jnp.bfloat16)
-
-        guarded(there, add)
-        push(
-            lambda target=target: paired.at[target], lambda: from_line.at[z],
-            lambda: line_sems.at[z], (target * 2 + y, txt), there,
-        )
+        for part in range(parts):
+            push_line(target, part, there)
 
     for device in others:
         arrived(lambda: from_txt.at[device[1]], lambda: term_sems.at[device[1]])
@@ -222,14 +257,18 @@
         image_sum += from_txt[device[1]].astype(jnp.float32)
     image_grad_ref[...] = image_sum
 
-    arrived(lambda: from_pair.at[z], lambda: pair_sems.at[z])
-    text_grad_ref[...] = pair_sum(z)
+    for part in range(parts):
+        pair_arrived(z, part)
+        text_grad_ref[pieces[part]] = pair_sum(z, part)
     for source, there in far_first[::-1]:
-        def add(source=source):
-            arrived(lambda: from_line.at[source], lambda: line_sems.at[source])
-            text_grad_ref[...] += from_line[source].astype(jnp.float32)
-
-        guarded(there, add)
+        for part in range(parts):
+            def add(source=source, part=part):
+                arrived(
+                    lambda: from_line.at[source, pieces[part]], lambda: line_sems.at[source, part]
+                )
+                text_grad_ref[pieces[part]] += from_line[source, pieces[part]].astype(jnp.float32)
+
+            guarded(there, add)
 
     for condition, copy in sent:
         guarded(condition, lambda: copy().wait_send())
@@ -240,10 +279,10 @@
     length = n_img // 2
     image_rows = labels.shape[0]
     vmem = pl.BlockSpec(memory_space=pltpu.VMEM)
-    hbm = pl.BlockSpec(memory_space=pl.ANY)
+    hbm = pl.BlockSpec(memory_space=pltpu.HBM)
     low = jnp.bfloat16
     dma = pltpu.SemaphoreType.DMA
-    sends = 3 + n_txt + 4 * length + 2 * (n_txt - 1) + 4 * length + n_txt
+    sends = parts * (6 + 10 * length) + 3 * n_txt
     loss, image_grad, text_grad = pl.pallas_call(
         functools.partial(kernel, n_img, n_txt),
         out_shape=(
@@ -251,9 +290,10 @@
             jax.ShapeDtypeStruct((rows, width), jnp.float32),
             jax.ShapeDtypeStruct((rows, width), jnp.float32),
         ),
-        in_specs=[vmem, hbm, hbm],
+        in_specs=[hbm, hbm, hbm],
         out_specs=(vmem, vmem, vmem),
         scratch_shapes=[
+            pltpu.VMEM((1, image_rows), jnp.int32),
             pltpu.VMEM((rows, width), jnp.float32),
             pltpu.VMEM((rows, width), jnp.float32),
             pltpu.VMEM((n_txt, rows, width), low),
@@ -265,13 +305,13 @@
             pltpu.VMEM((length, rows, width), low),
             pltpu.VMEM((n_txt, rows, width), low),
             pltpu.VMEM((n_txt, rows, width), low),
-            dma((2,)),
+            dma((3,)),
             dma((sends,)),
-            dma((2, length)),
+            dma((2, length, parts)),
             dma((n_txt,)),
             dma((n_txt,)),
-            dma((length,)),
-            dma((length,)),
+            dma((length, parts)),
+            dma((length, parts)),
             dma((n_txt,)),
         ],
         compiler_params=pltpu.CompilerParams(

time: 36.3 us -> 34.7 us (0.956)
  Pallas kernels: 31.2 us -> 29.6 us
    pallas_call x1, Pallas kernels: 31.2 us -> 29.6 us  [local(): pl.pallas_call(functools.partial(kernel, n_img, n_txt), out_shape=(jax.Sh...]
where the time goes in v2:
time: 34.7 us; the launch traced here: 34.5 us
  Pallas kernels  29.6 us (85%)
  local copies, waits for them, and re-layouts  4.28 us (12%)
  between operations  0.65 us (2%)
    pallas_call x1, Pallas kernels, local(): pl.pallas_call(functools.partial(kernel, n_img, n_txt), out_shape=(jax.Sh...  29.6 us
    unnamed x9, local copies, waits for them, and re-layouts  4.28 us

profile of v2, /device:TPU:0, one launch (start us, length us, event | category | flops | bytes accessed | tf_op | source)
XLA Modules:
  0.0 34.5 jit_solution(6281918264907155109)
XLA Ops:
  0.6 0.0 copy-start.2
  0.6 0.6 %copy-done.2 = s32[128]{0:T(128)S(1)} copy-done((s32[128]{0:T(128)S(1)}, s32[128]{0:T(128)}, u32[]{:S(2)}) %copy-start.2) | copy-done | bytes 536
  1.3 0.0 copy-start
  1.3 0.9 %copy-done = f32[32,1024]{1,0:T(8,128)S(1)} copy-done((f32[32,1024]{1,0:T(8,128)S(1)}, f32[32,1024]{1,0:T(8,128)}, u32[]{:S(2)}) %copy-start) | copy-done | bytes 131096
  2.2 0.0 copy-start.1
  2.2 0.9 %copy-done.1 = f32[32,1024]{1,0:T(8,128)S(1)} copy-done((f32[32,1024]{1,0:T(8,128)S(1)}, f32[32,1024]{1,0:T(8,128)}, u32[]{:S(2)}) %copy-start.1) | copy-done | bytes 131096
  3.1 29.6 %shard_map.58 = (f32[1,128]{1,0:T(1,128)S(1)}, f32[32,1024]{1,0:T(8,128)S(1)}, f32[32,1024]{1,0:T(8,128)S(1)}) custom-call(s32[1,128]{1,0:T(1,128)S(1)} %bitcast.2, f32[32,1024]{1,0:T(8,128)S(1)} %copy-done, f32[32,1024]{1,0:T(8,128)S(1)} %copy-done.1), custom_call_target="tpu_custom_call" | custom-call | tf_op jit(solution)/shard_map/pallas_call | solution.py:286
  32.7 0.5 %copy.9 = f32[128]{0:T(128)} copy(f32[128]{0:T(128)S(1)} %bitcast.3) | data formatting | bytes 1024
  33.2 0.7 %copy.10 = f32[32,1024]{1,0:T(8,128)} copy(f32[32,1024]{1,0:T(8,128)S(1)} %get-tuple-element.13) | data formatting | bytes 262144
  33.9 0.7 %copy.11 = f32[32,1024]{1,0:T(8,128)} copy(f32[32,1024]{1,0:T(8,128)S(1)} %get-tuple-element.14) | data formatting | bytes 262144
Async XLA Ops:
  0.6 0.7 %copy-start.2 = (s32[128]{0:T(128)S(1)}, s32[128]{0:T(128)}, u32[]{:S(2)}) copy-start(s32[128]{0:T(128)} %param.5) | copy-start | bytes 1540
  1.3 0.9 %copy-start = (f32[32,1024]{1,0:T(8,128)S(1)}, f32[32,1024]{1,0:T(8,128)}, u32[]{:S(2)}) copy-start(f32[32,1024]{1,0:T(8,128)} %images_hbm.1) | copy-start | bytes 393220
  2.2 0.9 %copy-start.1 = (f32[32,1024]{1,0:T(8,128)S(1)}, f32[32,1024]{1,0:T(8,128)}, u32[]{:S(2)}) copy-start(f32[32,1024]{1,0:T(8,128)} %texts_hbm.1) | copy-start | bytes 393220

commit v3 on v1

v3 whole, which is shorter than its diff:
```python
import functools

import jax
import jax.numpy as jnp
from jax import lax
from jax.experimental import pallas as pl
from jax.experimental.pallas import tpu as pltpu
from jax.sharding import PartitionSpec as P

logit_scale = 100.0
MESH = pl.DeviceIdType.MESH
parts = 2


def kernel(
    n_img, n_txt,
    labels_hbm, images_hbm, texts_hbm,
    loss_ref, image_grad_ref, text_grad_ref,
    labels_ref, images_in, texts_in, img_panel, txt_panel, stats, text_terms, from_line,
    image_terms, from_plane,
    load_sems, send_sems, txt_sems, img_sems, label_sems, stat_sems, line_sems, plane_sems,
):
    length = n_img // 2
    rows, width = images_in.shape
    img, txt = lax.axis_index("img"), lax.axis_index("txt")
    z, y = img // 2, img % 2
    c = txt % 2
    flip = 1 - y
    across = (z * 2 + flip, txt)
    beside = txt - c + (1 - c)
    partner = (img, beside)
    piece = width // parts
    pieces = [pl.ds(part * piece, piece) for part in range(parts)]
    groups = [lax.rem(txt + 2 * k, n_txt) for k in range(1, n_txt // 2)]
    ways = []
    for way in (1, -1):
        ways.append((way, jnp.logical_and(z + way >= 0, z + way < length)))

    barrier = pltpu.get_barrier_semaphore()

    def greet(device):
        pl.semaphore_signal(barrier, inc=1, device_id=device, device_id_type=MESH)

    for device in [across, partner] + [(img, group) for group in groups]:
        greet(device)
    greeted = 2 + len(groups)
    for way, inside in ways:
        greeted += jnp.where(inside, 1, 0)
        pl.when(inside)(lambda: greet(((z + way) * 2 + y, txt)))

    loads = [
        pltpu.make_async_copy(texts_hbm, texts_in, load_sems.at[0]),
        pltpu.make_async_copy(images_hbm, images_in, load_sems.at[1]),
        pltpu.make_async_copy(labels_hbm, labels_ref.at[y], load_sems.at[2]),
    ]
    for load in loads:
        load.start()
    loads[0].wait()
    txt_panel[z] = texts_in[...].astype(jnp.bfloat16)
    loads[1].wait()
    img_panel[y, txt] = images_in[...].astype(jnp.bfloat16)
    loads[2].wait()
    pl.semaphore_wait(barrier, greeted)

    sent = []

    def guarded(condition, act):
        if condition is None:
            act()
        else:
            pl.when(condition)(act)

    def push(src, dst, arrival, device, condition=None):
        number = len(sent)

        def copy():
            return pltpu.make_async_remote_copy(
                src_ref=src(), dst_ref=dst(), send_sem=send_sems.at[number], recv_sem=arrival(),
                device_id=device, device_id_type=MESH,
            )

        sent.append((condition, copy))
        guarded(condition, lambda: copy().start())

    def arrived(ref, arrival, condition=None):
        def act():
            pltpu.make_async_remote_copy(
                src_ref=ref(), dst_ref=ref(), send_sem=send_sems.at[0], recv_sem=arrival(),
                device_id=across, device_id_type=MESH,
            ).wait_recv()

        guarded(condition, act)

    def same(ref, arrival, device, condition=None):
        push(ref, ref, arrival, device, condition)

    def text_at(source, part):
        return (lambda: txt_panel.at[source, :, pieces[part]], lambda: txt_sems.at[source, part])

    def image_at(side, source, part):
        return (
            lambda: img_panel.at[side, source, :, pieces[part]],
            lambda: img_sems.at[side, source, part],
        )

    for part in range(parts):
        for way, inside in ways:
            same(*text_at(z, part), ((z + way) * 2 + y, txt), inside)
        same(*image_at(y, txt, part), across)
        for group in groups:
            same(*image_at(y, txt, part), (img, group))
    same(lambda: labels_ref.at[y], lambda: label_sems.at[y], across)
    for part in range(parts):
        same(*image_at(y, txt, part), partner)

    def pass_text(step):
        for part in range(parts):
            for way, inside in ways:
                source = z - way * step
                there = jnp.logical_and(source >= 0, source < length)
                arrived(*text_at(source, part), there)
                same(
                    *text_at(source, part), ((z + way) * 2 + y, txt),
                    jnp.logical_and(there, inside),
                )

    def pass_images():
        for part in range(parts):
            arrived(*image_at(flip, txt, part))
            if part < parts // 2:
                for group in groups:
                    same(*image_at(flip, txt, part), (img, group))
            for group in groups:
                arrived(*image_at(y, group, part))
                if part >= parts // 2:
                    same(*image_at(y, group, part), across)
            same(*image_at(flip, txt, part), partner)
            for group in groups:
                same(*image_at(y, group, part), partner)

    for step in range(1, length):
        pass_text(step)
        if step == 1:
            pass_images()
        if step == 2 or length == 2:
            for group in groups:
                for part in range(parts):
                    arrived(*image_at(flip, group, part))
                    same(*image_at(flip, group, part), partner)
    others = [lax.rem(beside + 2 * k, n_txt) for k in range(n_txt // 2)]
    for source in others:
        for part in range(parts):
            for side in range(2):
                arrived(*image_at(side, source, part))
    arrived(lambda: labels_ref.at[flip], lambda: label_sems.at[flip])

    text_rows, image_rows = length * rows, n_txt * rows
    image_low = img_panel[...].reshape(2 * image_rows, width)
    text_low = txt_panel[...].reshape(text_rows, width)
    logits = logit_scale * lax.dot_general(
        text_low, image_low, (((1,), (1,)), ((), ())), preferred_element_type=jnp.float32
    )
    place = lax.broadcasted_iota(jnp.int32, (text_rows, 1), 0)
    column = txt * (n_img * rows) + ((place // rows) * 2 + y) * rows + place % rows
    hits = column == jnp.concatenate([labels_ref[0], labels_ref[1]], axis=1)
    highest = jnp.max(logits, axis=0, keepdims=True)
    exp_total = jnp.sum(jnp.exp(logits - highest), axis=0, keepdims=True)
    positive = jnp.sum(jnp.where(hits, logits, 0.0), axis=0, keepdims=True)
    line = lax.broadcasted_iota(jnp.int32, stats.shape[2:], 0)
    stats[y, txt] = jnp.where(
        line == 0, highest, jnp.where(line == 1, exp_total, jnp.where(line == 2, positive, 0.0))
    )
    plane = [(flip, group) for group in groups] + [(flip, source) for source in others]
    plane += [(flip, txt)] + [(y, group) for group in groups] + [(y, source) for source in others]
    for side, source in plane:
        same(
            lambda: stats.at[y, txt], lambda: stat_sems.at[y, txt], (z * 2 + side, source)
        )
    for side, source in plane:
        arrived(lambda: stats.at[side, source], lambda: stat_sems.at[side, source])
    every = stats[...].reshape(2 * n_txt, 8, 2 * image_rows)
    tops = every[:, 0:1, :]
    top = jnp.max(tops, axis=0)
    total = jnp.sum(every[:, 1:2, :] * jnp.exp(tops - top[None]), axis=0)
    log_total = top + jnp.log(total)
    grad_tile = (
        logit_scale * (jnp.exp(logits - log_total) - hits.astype(jnp.float32))
    ).astype(jnp.bfloat16)

    far_first = []
    for step in range(length - 1, 0, -1):
        for target in (z + step, z - step):
            far_first.append((target, jnp.logical_and(target >= 0, target < length)))
    text_terms[...] = (
        jnp.dot(grad_tile, image_low, preferred_element_type=jnp.float32)
        .astype(jnp.bfloat16)
        .reshape(length, rows, width)
    )
    for target, there in far_first:
        push(
            lambda target=target: text_terms.at[target], lambda: from_line.at[z],
            lambda: line_sems.at[z], (target * 2 + y, txt), there,
        )
    image_terms[...] = (
        lax.dot_general(
            grad_tile, text_low, (((0,), (0,)), ((), ())), preferred_element_type=jnp.float32
        )
        .astype(jnp.bfloat16)
        .reshape(2, n_txt, rows, width)
    )
    for side, target in plane:
        push(
            lambda side=side, target=target: image_terms.at[side, target],
            lambda: from_plane.at[y, txt], lambda: plane_sems.at[y, txt], (z * 2 + side, target),
        )

    losses = log_total - jnp.sum(every[:, 2:3, :], axis=0)
    loss_ref[...] = jnp.where(y == 0, losses[:, :image_rows], losses[:, image_rows:])
    text_grad_ref[...] = text_terms[z].astype(jnp.float32)
    image_grad_ref[...] = image_terms[y, txt].astype(jnp.float32)

    def add_text(source):
        arrived(lambda: from_line.at[source], lambda: line_sems.at[source])
        text_grad_ref[...] += from_line[source].astype(jnp.float32)

    def add_image(side, source):
        arrived(lambda: from_plane.at[side, source], lambda: plane_sems.at[side, source])
        image_grad_ref[...] += from_plane[side, source].astype(jnp.float32)

    for side, source in plane[::-1]:
        add_image(side, source)
    for source, there in far_first[::-1]:
        pl.when(there)(lambda: add_text(source))

    for condition, copy in sent:
        guarded(condition, lambda: copy().wait_send())


def local(n_img, n_txt, images, texts, labels):
    rows, width = images.shape
    length = n_img // 2
    image_rows = labels.shape[0]
    vmem = pl.BlockSpec(memory_space=pltpu.VMEM)
    hbm = pl.BlockSpec(memory_space=pltpu.HBM)
    low = jnp.bfloat16
    dma = pltpu.SemaphoreType.DMA
    sends = parts * (3 * length + 4 * n_txt) + 5 * n_txt + 2 * length
    loss, image_grad, text_grad = pl.pallas_call(
        functools.partial(kernel, n_img, n_txt),
        out_shape=(
            jax.ShapeDtypeStruct((1, image_rows), jnp.float32),
            jax.ShapeDtypeStruct((rows, width), jnp.float32),
            jax.ShapeDtypeStruct((rows, width), jnp.float32),
        ),
        in_specs=[hbm, hbm, hbm],
        out_specs=(vmem, vmem, vmem),
        scratch_shapes=[
            pltpu.VMEM((2, 1, image_rows), jnp.int32),
            pltpu.VMEM((rows, width), jnp.float32),
            pltpu.VMEM((rows, width), jnp.float32),
            pltpu.VMEM((2, n_txt, rows, width), low),
            pltpu.VMEM((length, rows, width), low),
            pltpu.VMEM((2, n_txt, 8, 2 * image_rows), jnp.float32),
            pltpu.VMEM((length, rows, width), low),
            pltpu.VMEM((length, rows, width), low),
            pltpu.VMEM((2, n_txt, rows, width), low),
            pltpu.VMEM((2, n_txt, rows, width), low),
            dma((3,)),
            dma((sends,)),
            dma((length, parts)),
            dma((2, n_txt, parts)),
            dma((2,)),
            dma((2, n_txt)),
            dma((length,)),
            dma((2, n_txt)),
        ],
        compiler_params=pltpu.CompilerParams(
            collective_id=0, has_side_effects=True, vmem_limit_bytes=48 * 1024 * 1024
        ),
    )(labels.reshape(1, image_rows), images, texts)
    return loss.reshape(image_rows), image_grad, text_grad


def solution(mesh):
    in_specs = (P(("img", "txt"), None), P(("txt", "img"), None), P("img"))
    out_specs = (P("img"), P(("img", "txt"), None), P(("txt", "img"), None))
    body = functools.partial(local, mesh.shape["img"], mesh.shape["txt"])
    return jax.shard_map(body, mesh=mesh, in_specs=in_specs, out_specs=out_specs, check_vma=False)
```

time: 36.3 us -> 32.4 us (0.89)
  Pallas kernels: 31.2 us -> 27.3 us
    pallas_call x1, Pallas kernels: 31.2 us -> 27.3 us  [local(): pl.pallas_call(functools.partial(kernel, n_img, n_txt), out_shape=(jax.Sh...]
where the time goes in v3:
time: 32.4 us; the launch traced here: 32.2 us
  Pallas kernels  27.3 us (84%)
  local copies, waits for them, and re-layouts  4.28 us (13%)
  between operations  0.65 us (2%)
    pallas_call x1, Pallas kernels, local(): pl.pallas_call(functools.partial(kernel, n_img, n_txt), out_shape=(jax.Sh...  27.3 us
    unnamed x9, local copies, waits for them, and re-layouts  4.28 us

profile of v3, /device:TPU:0, one launch (start us, length us, event | category | flops | bytes accessed | tf_op | source)
XLA Modules:
  0.0 32.2 jit_solution(4759387238368365761)
XLA Ops:
  0.6 0.0 copy-start.2
  0.6 0.6 %copy-done.2 = s32[128]{0:T(128)S(1)} copy-done((s32[128]{0:T(128)S(1)}, s32[128]{0:T(128)}, u32[]{:S(2)}) %copy-start.2) | copy-done | bytes 536
  1.3 0.0 copy-start
  1.3 0.9 %copy-done = f32[32,1024]{1,0:T(8,128)S(1)} copy-done((f32[32,1024]{1,0:T(8,128)S(1)}, f32[32,1024]{1,0:T(8,128)}, u32[]{:S(2)}) %copy-start) | copy-done | bytes 131096
  2.2 0.0 copy-start.1
  2.2 0.9 %copy-done.1 = f32[32,1024]{1,0:T(8,128)S(1)} copy-done((f32[32,1024]{1,0:T(8,128)S(1)}, f32[32,1024]{1,0:T(8,128)}, u32[]{:S(2)}) %copy-start.1) | copy-done | bytes 131096
  3.1 27.3 %shard_map.58 = (f32[1,128]{1,0:T(1,128)S(1)}, f32[32,1024]{1,0:T(8,128)S(1)}, f32[32,1024]{1,0:T(8,128)S(1)}) custom-call(s32[1,128]{1,0:T(1,128)S(1)} %bitcast.2, f32[32,1024]{1,0:T(8,128)S(1)} %copy-done, f32[32,1024]{1,0:T(8,128)S(1)} %copy-done.1), custom_call_target="tpu_custom_call" | custom-call | tf_op jit(solution)/shard_map/pallas_call | solution.py:248
  30.4 0.5 %copy.9 = f32[128]{0:T(128)} copy(f32[128]{0:T(128)S(1)} %bitcast.3) | data formatting | bytes 1024
  30.9 0.7 %copy.10 = f32[32,1024]{1,0:T(8,128)} copy(f32[32,1024]{1,0:T(8,128)S(1)} %get-tuple-element.13) | data formatting | bytes 262144
  31.6 0.7 %copy.11 = f32[32,1024]{1,0:T(8,128)} copy(f32[32,1024]{1,0:T(8,128)S(1)} %get-tuple-element.14) | data formatting | bytes 262144
Async XLA Ops:
  0.6 0.7 %copy-start.2 = (s32[128]{0:T(128)S(1)}, s32[128]{0:T(128)}, u32[]{:S(2)}) copy-start(s32[128]{0:T(128)} %param.5) | copy-start | bytes 1540
  1.3 0.9 %copy-start = (f32[32,1024]{1,0:T(8,128)S(1)}, f32[32,1024]{1,0:T(8,128)}, u32[]{:S(2)}) copy-start(f32[32,1024]{1,0:T(8,128)} %images_hbm.1) | copy-start | bytes 393220
  2.2 0.9 %copy-start.1 = (f32[32,1024]{1,0:T(8,128)S(1)}, f32[32,1024]{1,0:T(8,128)}, u32[]{:S(2)}) copy-start(f32[32,1024]{1,0:T(8,128)} %texts_hbm.1) | copy-start | bytes 393220

commit v4 on v3

--- a/solution.py
+++ b/solution.py
@@ -9,6 +9,7 @@
 
 logit_scale = 100.0
 MESH = pl.DeviceIdType.MESH
+farthest = 3
 parts = 2
 
 
@@ -18,7 +19,7 @@
     loss_ref, image_grad_ref, text_grad_ref,
     labels_ref, images_in, texts_in, img_panel, txt_panel, stats, text_terms, from_line,
     image_terms, from_plane,
-    load_sems, send_sems, txt_sems, img_sems, label_sems, stat_sems, line_sems, plane_sems,
+    load_sems, send_sems, near_sems, txt_sems, img_sems, label_sems, stat_sems, line_sems, plane_sems,
 ):
     length = n_img // 2
     rows, width = images_in.shape
@@ -103,9 +104,34 @@
             lambda: img_sems.at[side, source, part],
         )
 
+    def place_in(offset):
+        return jnp.logical_and(z + offset >= 0, z + offset < length)
+
+    def tell(reach):
+        for way in (1, -1):
+            @pl.when(jnp.logical_and(place_in(way * (reach - 1)), place_in(-way)))
+            def _():
+                pl.semaphore_signal(
+                    near_sems.at[(1 - way) // 2, reach - 1], inc=1,
+                    device_id=((z - way) * 2 + y, txt), device_id_type=MESH,
+                )
+
+    def told(reach):
+        for way in (1, -1):
+            @pl.when(place_in(way * reach))
+            def _():
+                pl.semaphore_wait(near_sems.at[(1 - way) // 2, reach - 1], 1)
+
+    def text_to(source, part, offset, there=None):
+        inside = place_in(offset)
+        if there is not None:
+            inside = jnp.logical_and(inside, there)
+        same(*text_at(source, part), ((z + offset) * 2 + y, txt), inside)
+
+    tell(2)
     for part in range(parts):
-        for way, inside in ways:
-            same(*text_at(z, part), ((z + way) * 2 + y, txt), inside)
+        for way in (1, -1):
+            text_to(z, part, way)
         same(*image_at(y, txt, part), across)
         for group in groups:
             same(*image_at(y, txt, part), (img, group))
@@ -113,16 +139,24 @@
     for part in range(parts):
         same(*image_at(y, txt, part), partner)
 
+    for reach in range(2, farthest + 1):
+        told(reach)
+        if reach < farthest:
+            tell(reach + 1)
+        for part in range(parts):
+            for way in (1, -1):
+                text_to(z, part, way * reach)
+
     def pass_text(step):
         for part in range(parts):
-            for way, inside in ways:
+            for way in (1, -1):
                 source = z - way * step
-                there = jnp.logical_and(source >= 0, source < length)
+                there = place_in(-way * step)
                 arrived(*text_at(source, part), there)
-                same(
-                    *text_at(source, part), ((z + way) * 2 + y, txt),
-                    jnp.logical_and(there, inside),
-                )
+                if step % farthest == 0:
+                    for reach in range(1, farthest + 1):
+                        if step + reach < length:
+                            text_to(source, part, way * reach, there)
 
     def pass_images():
         for part in range(parts):
@@ -244,7 +278,7 @@
     hbm = pl.BlockSpec(memory_space=pltpu.HBM)
     low = jnp.bfloat16
     dma = pltpu.SemaphoreType.DMA
-    sends = parts * (3 * length + 4 * n_txt) + 5 * n_txt + 2 * length
+    sends = parts * (4 * length + 4 * n_txt + 2 * farthest) + 5 * n_txt + 2 * length
     loss, image_grad, text_grad = pl.pallas_call(
         functools.partial(kernel, n_img, n_txt),
         out_shape=(
@@ -267,6 +301,7 @@
             pltpu.VMEM((2, n_txt, rows, width), low),
             dma((3,)),
             dma((sends,)),
+            pltpu.SemaphoreType.REGULAR((2, farthest)),
             dma((length, parts)),
             dma((2, n_txt, parts)),
             dma((2,)),
@@ -277,7 +312,7 @@
         compiler_params=pltpu.CompilerParams(
             collective_id=0, has_side_effects=True, vmem_limit_bytes=48 * 1024 * 1024
         ),
-    )(labels.reshape(1, image_rows), images, texts)
+    )(*[pltpu.with_memory_space_constraint(a, pltpu.HBM) for a in (labels.reshape(1, image_rows), images, texts)])
     return loss.reshape(image_rows), image_grad, text_grad
 
 

time: 32.4 us -> 28.7 us (0.89)
  local copies, waits for them, and re-layouts: 4.28 us -> 1.82 us
  Pallas kernels: 27.3 us -> 26.1 us
    unnamed x9 -> x3, local copies, waits for them, and re-layouts: 4.28 us -> 1.82 us
    pallas_call x1, Pallas kernels: 27.3 us -> 26.1 us  [local(): pl.pallas_call(functools.partial(kernel, n_img, n_txt), out_shape=(jax.Sh...]
where the time goes in v4:
time: 28.7 us; the launch traced here: 28.6 us
  Pallas kernels  26.1 us (91%)
  local copies, waits for them, and re-layouts  1.82 us (6%)
  between operations  0.64 us (2%)
    pallas_call x1, Pallas kernels, local(): pl.pallas_call(functools.partial(kernel, n_img, n_txt), out_shape=(jax.Sh...  26.1 us
    unnamed x3, local copies, waits for them, and re-layouts  1.82 us

profile of v4, /device:TPU:0, one launch (start us, length us, event | category | flops | bytes accessed | tf_op | source)
XLA Modules:
  0.0 28.6 jit_solution(11411921514073856492)
XLA Ops:
  0.6 26.1 %shard_map.58 = (f32[1,128]{1,0:T(1,128)S(1)}, f32[32,1024]{1,0:T(8,128)S(1)}, f32[32,1024]{1,0:T(8,128)S(1)}) custom-call(s32[1,128]{1,0:T(1,128)} %bitcast.3, f32[32,1024]{1,0:T(8,128)} %images_hbm.1, f32[32,1024]{1,0:T(8,128)} %texts_hbm.1), custom_call_target="tpu_custom_call" | custom-call | tf_op jit(solution)/shard_map/pallas_call | solution.py:282
  26.8 0.5 %copy.9 = f32[128]{0:T(128)} copy(f32[128]{0:T(128)S(1)} %bitcast.2) | data formatting | bytes 1024
  27.3 0.7 %copy.10 = f32[32,1024]{1,0:T(8,128)} copy(f32[32,1024]{1,0:T(8,128)S(1)} %get-tuple-element.13) | data formatting | bytes 262144
  27.9 0.7 %copy.11 = f32[32,1024]{1,0:T(8,128)} copy(f32[32,1024]{1,0:T(8,128)S(1)} %get-tuple-element.14) | data formatting | bytes 262144

commit v5 on v4

--- a/solution.py
+++ b/solution.py
@@ -10,7 +10,7 @@
 logit_scale = 100.0
 MESH = pl.DeviceIdType.MESH
 farthest = 3
-parts = 2
+parts = 1
 
 
 def kernel(

time: 28.7 us -> 28.3 us (0.986)
  Pallas kernels: 26.1 us -> 25.7 us
    pallas_call x1, Pallas kernels: 26.1 us -> 25.7 us  [local(): pl.pallas_call(functools.partial(kernel, n_img, n_txt), out_shape=(jax.Sh...]
where the time goes in v5:
time: 28.3 us; the launch traced here: 28.1 us
  Pallas kernels  25.7 us (91%)
  local copies, waits for them, and re-layouts  1.82 us (6%)
  between operations  0.64 us (2%)
    pallas_call x1, Pallas kernels, local(): pl.pallas_call(functools.partial(kernel, n_img, n_txt), out_shape=(jax.Sh...  25.7 us
    unnamed x3, local copies, waits for them, and re-layouts  1.82 us

profile of v5, /device:TPU:0, one launch (start us, length us, event | category | flops | bytes accessed | tf_op | source)
XLA Modules:
  0.0 28.1 jit_solution(1178930571300514437)
XLA Ops:
  0.6 25.7 %shard_map.58 = (f32[1,128]{1,0:T(1,128)S(1)}, f32[32,1024]{1,0:T(8,128)S(1)}, f32[32,1024]{1,0:T(8,128)S(1)}) custom-call(s32[1,128]{1,0:T(1,128)} %bitcast.3, f32[32,1024]{1,0:T(8,128)} %images_hbm.1, f32[32,1024]{1,0:T(8,128)} %texts_hbm.1), custom_call_target="tpu_custom_call" | custom-call | tf_op jit(solution)/shard_map/pallas_call | solution.py:282
  26.3 0.5 %copy.9 = f32[128]{0:T(128)} copy(f32[128]{0:T(128)S(1)} %bitcast.2) | data formatting | bytes 1024
  26.8 0.7 %copy.10 = f32[32,1024]{1,0:T(8,128)} copy(f32[32,1024]{1,0:T(8,128)S(1)} %get-tuple-element.13) | data formatting | bytes 262144
  27.5 0.7 %copy.11 = f32[32,1024]{1,0:T(8,128)} copy(f32[32,1024]{1,0:T(8,128)S(1)} %get-tuple-element.14) | data formatting | bytes 262144
